TPU v7x, 32 devices: a whole 2x2x4 slice. The times are simulated.
32 devices in a mesh: stack: 2 (over x), scene: 16 (over z, y, core).
Axes of the slice: x: 2, y: 2, z: 4, core: 2. Of those that a mesh axis runs over, the one named last changes fastest.
Arguments:
- raw_echoes: bfloat16 [4096, 2, 4, 512], P('scene', None, 'stack'), parts along dimension 2, may hold values from -6 to 6
- azimuth_phase: float32 [8192, 512], P('stack', 'scene'), parts along dimension 0, may hold values from -3.140625 to 3.140625
- band_offset: int32 [1024], P(('stack', 'scene')), parts along dimension 0, may hold values from 0 to 8, as said below
- partners: int32 [2, 2], P('stack'), parts along dimension 0, may hold values from 0 to 0, as said below
Outputs:
- goldstein: bfloat16 [4, 1024, 2, 512], P('stack', None, None, 'scene'), parts along dimension 0
There are 2 independent parts, one for each index of `stack`. A program takes and returns all parts, laid end to end along the dimension named above; each array names one. Nothing has to cross between parts.
Inputs may be any that keep to these rules, and one draw needn't show every extreme that they name: `partners`: row i names two dates that precede date i + 1, each from 0 to i, possibly equal; the last row's first entry is 0. `band_offset`: both 0 and 8 occur among the range bins.
All inputs are finite; a program needn't handle non-finite values.
Results may differ from a plain program's by a relative error of at most 0.023.
Values may be sent and summed in bfloat16 or wider, within the bound.
A program may use at most 128 MiB of HBM per device.

v0:
```python
import math

import jax
import jax.numpy as jnp
import numpy as np
from jax import lax
from jax.experimental import pallas as pl
from jax.experimental.pallas import tpu as pltpu
from jax.sharding import PartitionSpec as P

SPLIT = 64
LOOKS = 4
PATCH = 64
SHIFT = 8
TAPS = 2 * SHIFT - 1
EPSILON = 1e-06
STRIP = 32
GROUPS = STRIP // 2
LANES = 2 * SPLIT
CHUNKS = STRIP // 4
HALO_CHUNKS = CHUNKS // 2
VMEM_LIMIT = 56 * 1024 * 1024


def base_tables():
    k = np.arange(64)
    angle = 2.0 * np.pi * ((k[:, None] * k[None, :]) % 64) / 64.0
    return np.cos(angle), np.sin(angle)


def twiddle_tables():
    k = np.arange(SPLIT)
    angle = 2.0 * np.pi * ((k[:, None] * k[None, :]) % (SPLIT * SPLIT)) / (SPLIT * SPLIT)
    return (
        np.tile(np.cos(angle), (1, 2)).astype(np.float32),
        np.tile(np.sin(angle), (1, 2)).astype(np.float32),
    )


def bf16(table):
    return jnp.asarray(np.asarray(table, np.float32), jnp.bfloat16)


def left_table(direction):
    c, s = base_tables()
    return np.block([[c, direction * s], [-direction * s, c]])


def right_table(direction):
    c, s = base_tables()
    eye = np.eye(2)
    return np.block(
        [
            [np.kron(eye, c), np.kron(eye, -direction * s)],
            [np.kron(eye, direction * s), np.kron(eye, c)],
        ]
    )


def look_table():
    table = np.zeros((4, 2, 2, SPLIT, 2, 4, 2, SPLIT // LOOKS))
    for g in range(4):
        for c in range(2):
            for rb in range(2):
                for q in range(SPLIT):
                    table[g, c, rb, q, rb, g, c, q // LOOKS] = 1.0 / LOOKS
    return table.reshape(4 * 2 * 2 * SPLIT, 2 * 4 * 2 * SPLIT // LOOKS)


def patch_azimuth_table():
    c, s = base_tables()
    table = np.zeros((4, 4, 2, 16, 4, 2, 64))
    for p in range(4):
        part_c, part_s = c[16 * p : 16 * p + 16], s[16 * p : 16 * p + 16]
        for r in range(4):
            table[p, r, 0, :, r, 0] = part_c
            table[p, r, 1, :, r, 0] = part_s
            table[p, r, 0, :, r, 1] = -part_s
            table[p, r, 1, :, r, 1] = part_c
    return table.reshape(512, 512)


def patch_range_table():
    c, s = base_tables()
    return np.concatenate([c, s], axis=1)


def back_azimuth_table():
    c, s = base_tables()
    c, s = c[:, 16:48], s[:, 16:48]
    table = np.zeros((4, 2, 64, 2, 4, 32))
    for i in range(4):
        table[i, 0, :, 0, i] = c
        table[i, 1, :, 0, i] = -s
        table[i, 0, :, 1, i] = s
        table[i, 1, :, 1, i] = c
    return table.reshape(512, 256)


def back_range_table():
    c, s = base_tables()
    c, s = c[16:48], s[16:48]
    return np.block([[c, -s], [s, c]])


def whole(count):
    return [pl.BlockSpec(memory_space=pltpu.VMEM)] * count


def dot(a, b):
    return jnp.dot(a, b, preferred_element_type=jnp.float32)


def weights_kernel(band_ref, phase_ref, weight_ref, cos_ref, sin_ref):
    g = pl.program_id(0)
    shape = (SPLIT, LANES)
    lane = lax.broadcasted_iota(jnp.int32, shape, 1)
    row = lax.broadcasted_iota(jnp.int32, shape, 0)
    k = row + SPLIT * (lane & (SPLIT - 1))
    total = SPLIT * SPLIT
    f = jnp.where(k < total // 2, k, k - total).astype(jnp.float32)
    ratio = f * (2.0 / total)
    band = jnp.where(lane < SPLIT, band_ref[g], band_ref[g + GROUPS]).astype(jnp.float32)
    s = band * (ratio * ratio - 0.5)
    n = jnp.floor(s + 0.5)
    y = s - n
    y2 = y * y
    pi = math.pi
    poly = -(pi**11) / 39916800.0
    for power, fact in ((9, 362880.0), (7, -5040.0), (5, 120.0), (3, -6.0), (1, 1.0)):
        poly = poly * y2 + (pi**power) / fact
    odd = n.astype(jnp.int32) & 1
    lobe = jnp.where(odd == 1, 1.0, -1.0) * (y * poly) * (1.0 / pi)
    cos_s = 0.5 * jnp.cos(s * (pi / 4.0))
    sin_s = 0.5 * jnp.sin(s * (pi / 4.0))
    for tap in range(TAPS):
        m = tap + 1 - SHIFT
        x = m - s
        sign = 1.0 if m % 2 == 0 else -1.0
        safe = jnp.where(x == 0.0, 1.0, x)
        sinc = jnp.where(x == 0.0, 1.0, (sign * lobe) / safe)
        window = 0.5 + math.cos(pi * m / 4.0) * cos_s + math.sin(pi * m / 4.0) * sin_s
        weight_ref[0, tap] = jnp.where(jnp.abs(x) < SHIFT / 2.0, sinc * window, 0.0)
    cos_ref[0] = jnp.cos(phase_ref[0])
    sin_ref[0] = jnp.sin(phase_ref[0])


def make_weights(band, phase):
    block = pl.BlockSpec((1, SPLIT, LANES), lambda g: (g, 0, 0))
    plane = jax.ShapeDtypeStruct((GROUPS, SPLIT, LANES), jnp.float32)
    return pl.pallas_call(
        weights_kernel,
        grid=(GROUPS,),
        in_specs=[pl.BlockSpec(memory_space=pltpu.SMEM), block],
        out_specs=[
            pl.BlockSpec((1, TAPS, SPLIT, LANES), lambda g: (g, 0, 0, 0)),
            block,
            block,
        ],
        out_shape=[jax.ShapeDtypeStruct((GROUPS, TAPS, SPLIT, LANES), jnp.float32), plane, plane],
        cost_estimate=pl.CostEstimate(
            flops=60_000_000, bytes_accessed=10_000_000, transcendentals=600_000
        ),
        name="weights",
    )(band, phase)


def forward_kernel(x_ref, left_ref, right_ref, tc_ref, ts_ref, dop_ref, up_ref, down_ref):
    low = lax.broadcasted_iota(jnp.int32, (SPLIT, LANES), 1) < SPLIT
    for d in range(dop_ref.shape[0]):

        def body(i, carry):
            for half in range(2):
                g = i + half * (GROUPS // 2)
                start = pl.multiple_of((d * GROUPS + g) * LANES, LANES)
                first = dot(left_ref[...], x_ref[:, pl.ds(start, LANES)])
                re, im = first[:SPLIT], first[SPLIT:]
                tc, ts = tc_ref[...], ts_ref[...]
                segment = jnp.concatenate([re * tc + im * ts, im * tc - re * ts], axis=1)
                second = dot(segment.astype(jnp.bfloat16), right_ref[...]) * (1.0 / SPLIT)
                dop_ref[d, g] = second.astype(jnp.bfloat16)
                re, im = second[:, :LANES], second[:, LANES:]
                if half == 0:
                    edge = jnp.where(low, re, pltpu.roll(im, SPLIT, 1))
                    down_ref[d, i] = edge.astype(jnp.bfloat16)
                else:
                    edge = jnp.where(low, pltpu.roll(re, SPLIT, 1), im)
                    up_ref[d, i] = edge.astype(jnp.bfloat16)
            return carry

        lax.fori_loop(0, GROUPS // 2, body, 0, unroll=2)


def forward(x, dates, left):
    edge = jax.ShapeDtypeStruct((dates, SHIFT, SPLIT, LANES), jnp.bfloat16)
    tc, ts = twiddle_tables()
    return pl.pallas_call(
        forward_kernel,
        in_specs=whole(5),
        out_specs=whole(3),
        out_shape=[
            jax.ShapeDtypeStruct((dates, GROUPS, SPLIT, 2 * LANES), jnp.bfloat16),
            edge,
            edge,
        ],
        compiler_params=pltpu.CompilerParams(vmem_limit_bytes=VMEM_LIMIT),
        name="forward",
    )(x, bf16(left), bf16(right_table(1.0)), jnp.asarray(tc), jnp.asarray(ts))


def focus_kernel(
    dop_ref, before_ref, after_ref, weight_ref, cos_ref, sin_ref,
    right_ref, left_ref, tc_ref, ts_ref, look_ref, out_ref, ext_ref, high_ref, low_ref,
):
    low = lax.broadcasted_iota(jnp.int32, (SPLIT, LANES), 1) < SPLIT
    dates = dop_ref.shape[0]
    for d in range(dates):

        def fill(i, carry):
            own = dop_ref[d, i].astype(jnp.float32)
            top = dop_ref[d, i + SHIFT].astype(jnp.float32)
            before = before_ref[d, i].astype(jnp.float32)
            after = after_ref[d, i].astype(jnp.float32)
            before_parts = (before, pltpu.roll(before, SPLIT, 1))
            after_parts = (pltpu.roll(after, SPLIT, 1), after)
            for c in range(2):
                mine = own[:, c * LANES : (c + 1) * LANES]
                upper = top[:, c * LANES : (c + 1) * LANES]
                ext_ref[d, c, i + SHIFT] = mine
                ext_ref[d, c, i + 2 * SHIFT] = upper
                ext_ref[d, c, i] = jnp.where(low, before_parts[c], pltpu.roll(upper, SPLIT, 1))
                ext_ref[d, c, i + 3 * SHIFT] = jnp.where(
                    low, pltpu.roll(mine, SPLIT, 1), after_parts[c]
                )
            return carry

        lax.fori_loop(0, SHIFT, fill, 0)

    def body(g, carry):
        parts = []
        for half in range(2):
            rows = pl.ds(half * (SPLIT // 2), SPLIT // 2)
            sums = [jnp.zeros((SPLIT // 2, LANES), jnp.float32) for _ in range(2 * dates)]
            for tap in range(TAPS):
                weight = weight_ref[g, tap, rows]
                for d in range(dates):
                    for c in range(2):
                        sums[2 * d + c] += weight * ext_ref[d, c, g + tap + 1, rows]
            cos_phase, sin_phase = cos_ref[g, rows], sin_ref[g, rows]
            parts.append(
                [
                    jnp.concatenate(
                        [
                            sums[2 * d] * cos_phase - sums[2 * d + 1] * sin_phase,
                            sums[2 * d + 1] * cos_phase + sums[2 * d] * sin_phase,
                        ],
                        axis=1,
                    ).astype(jnp.bfloat16)
                    for d in range(dates)
                ]
            )
        focused = []
        for d in range(dates):
            compressed = jnp.concatenate([parts[0][d], parts[1][d]], axis=0)
            first = dot(compressed, right_ref[...])
            re, im = first[:, :LANES], first[:, LANES:]
            tc, ts = tc_ref[...], ts_ref[...]
            segment = jnp.concatenate([re * tc - im * ts, im * tc + re * ts], axis=0)
            second = dot(left_ref[...], segment.astype(jnp.bfloat16)) * (1.0 / SPLIT)
            second = second.astype(jnp.bfloat16).astype(jnp.float32)
            focused.append((second[:SPLIT], second[SPLIT:]))
        (tr, ti), (lr, li) = focused
        product = jnp.concatenate([lr * tr + li * ti, li * tr - lr * ti], axis=1)
        high = product.astype(jnp.bfloat16)
        high_ref[g] = high
        low_ref[g] = (product - high.astype(jnp.float32)).astype(jnp.bfloat16)
        return carry

    lax.fori_loop(0, GROUPS, body, 0)
    for big in range(GROUPS // 4):
        high = jnp.concatenate([high_ref[4 * big + j] for j in range(4)], axis=1)
        rest = jnp.concatenate([low_ref[4 * big + j] for j in range(4)], axis=1)
        looked = dot(high, look_ref[...]) + dot(rest, look_ref[...])
        out_ref[big] = looked[:, :LANES].astype(jnp.bfloat16)
        out_ref[HALO_CHUNKS + big] = looked[:, LANES:].astype(jnp.bfloat16)


def focus(dop, before, after, weight, cos_phase, sin_phase):
    dates = dop.shape[0]
    tc, ts = twiddle_tables()
    return pl.pallas_call(
        focus_kernel,
        in_specs=whole(11),
        out_specs=pl.BlockSpec(memory_space=pltpu.VMEM),
        out_shape=jax.ShapeDtypeStruct((CHUNKS, SPLIT, LANES), jnp.bfloat16),
        scratch_shapes=[
            pltpu.VMEM((dates, 2, GROUPS + 2 * SHIFT, SPLIT, LANES), jnp.float32),
            pltpu.VMEM((GROUPS, SPLIT, 2 * LANES), jnp.bfloat16),
            pltpu.VMEM((GROUPS, SPLIT, 2 * LANES), jnp.bfloat16),
        ],
        compiler_params=pltpu.CompilerParams(vmem_limit_bytes=VMEM_LIMIT),
        name="focus",
    )(
        dop, before, after, weight, cos_phase, sin_phase,
        bf16(right_table(-1.0)), bf16(left_table(-1.0)),
        jnp.asarray(tc), jnp.asarray(ts), bf16(look_table()),
    )


def filter_kernel(
    own_ref, before_ref, after_ref, azimuth_ref, range_ref, back_azimuth_ref, back_range_ref,
    out_ref, line_ref, grid_ref,
):
    patches = SPLIT // 2
    line_ref[...] = jnp.zeros(line_ref.shape, jnp.float32)
    for j in range(HALO_CHUNKS):
        line_ref[j, pl.ds(1, SPLIT)] = before_ref[j].astype(jnp.float32)
        line_ref[HALO_CHUNKS + CHUNKS + j, pl.ds(1, SPLIT)] = after_ref[j].astype(jnp.float32)
    for j in range(CHUNKS):
        line_ref[HALO_CHUNKS + j, pl.ds(1, SPLIT)] = own_ref[j].astype(jnp.float32)

    def forward_lines(step, carry):
        rows = []
        for j in range(4):
            chunk = 4 * step + j
            rows.append(
                jnp.concatenate(
                    [line_ref[chunk, pl.ds(p, patches, stride=2)] for p in range(4)], axis=1
                )
            )
        lines = jnp.concatenate(rows, axis=0).astype(jnp.bfloat16)
        result = dot(lines, azimuth_ref[...]).astype(jnp.bfloat16).astype(jnp.float32)
        for j in range(4):
            for r in range(4):
                start = pl.multiple_of(((4 * step + j) * 4 + r) * patches, patches)
                grid_ref[pl.ds(start, patches)] = result[
                    j * patches : (j + 1) * patches, r * LANES : (r + 1) * LANES
                ]
        return carry

    lax.fori_loop(0, (2 * HALO_CHUNKS + CHUNKS) // 4, forward_lines, 0)
    sign = jnp.where(lax.broadcasted_iota(jnp.int32, (PATCH, LANES), 1) < PATCH, 1.0, -1.0)

    def filter_patches(step, carry):
        tiles = []
        for j in range(4):
            tile = grid_ref[pl.ds(4 * step + j, PATCH, stride=patches)]
            swapped = pltpu.roll(tile, PATCH, 1) * sign
            tiles.append(jnp.concatenate([tile, swapped], axis=0).astype(jnp.bfloat16))
        spectra = dot(range_ref[...], jnp.concatenate(tiles, axis=1)) * (1.0 / PATCH)
        kept = []
        for j in range(4):
            spectrum = spectra[:, j * LANES : (j + 1) * LANES]
            power = spectrum * spectrum
            magnitude = jnp.sqrt(power + pltpu.roll(power, PATCH, 1) + EPSILON)
            row_sum = (
                magnitude
                + pltpu.roll(magnitude, 1, 0)
                + pltpu.roll(magnitude, PATCH - 1, 0)
            )
            smooth = (row_sum + pltpu.roll(row_sum, 1, 1) + pltpu.roll(row_sum, LANES - 1, 1)) * (
                1.0 / 9.0
            )
            level = jnp.sum(jnp.sum(magnitude, axis=0, keepdims=True), axis=1, keepdims=True)
            level = level * (1.0 / (PATCH * LANES)) + EPSILON
            kept.append((spectrum * (smooth / level)).astype(jnp.bfloat16))
        back = dot(jnp.concatenate(kept, axis=1), back_azimuth_ref[...]).astype(jnp.bfloat16)
        stacked = jnp.concatenate([back[:, :LANES], back[:, LANES:]], axis=0)
        result = (dot(back_range_ref[...], stacked) * (1.0 / PATCH)).astype(jnp.bfloat16)
        start = pl.multiple_of(step * LANES, LANES)
        for pair in range(out_ref.shape[0]):
            out_ref[pair, :, pl.ds(start, LANES)] = result
        return carry

    lax.fori_loop(0, patches // 4, filter_patches, 0)


def filtered(own, before, after, pairs):
    looks = SPLIT * SPLIT // LOOKS
    return pl.pallas_call(
        filter_kernel,
        in_specs=whole(7),
        out_specs=pl.BlockSpec(memory_space=pltpu.VMEM),
        out_shape=jax.ShapeDtypeStruct((pairs, 2 * STRIP, looks), jnp.bfloat16),
        scratch_shapes=[
            pltpu.VMEM((2 * CHUNKS, SPLIT + 8, LANES), jnp.float32),
            pltpu.VMEM((PATCH * SPLIT // 2, LANES), jnp.float32),
        ],
        compiler_params=pltpu.CompilerParams(vmem_limit_bytes=VMEM_LIMIT),
        name="filter",
    )(
        own, before, after,
        bf16(patch_azimuth_table()), bf16(patch_range_table()),
        bf16(back_azimuth_table()), bf16(back_range_table()),
    )


def shifted(last, initial, axis):
    count = lax.axis_size(axis)
    up = [(i, i + 1) for i in range(count - 1)]
    down = [(j, i) for i, j in up]
    return lax.ppermute(last, axis, up), lax.ppermute(initial, axis, down)


def on_device(raw_echoes, azimuth_phase, band_offset, partners):
    scene = lax.axis_size("scene")
    dates = raw_echoes.shape[2]
    local = raw_echoes.shape[0] // SPLIT
    pairs = partners.size
    assert dates == 2 and raw_echoes.shape[3] == scene * STRIP
    pieces = raw_echoes.reshape(local, SPLIT, 2, dates, scene, 2, GROUPS)
    pieces = pieces.transpose(4, 2, 0, 3, 6, 5, 1).reshape(
        scene, 2 * local, dates * GROUPS * LANES
    )
    arrived = lax.all_to_all(pieces, "scene", split_axis=0, concat_axis=0, tiled=True)
    arrived = arrived.reshape(2 * SPLIT, dates * GROUPS * LANES)
    left = left_table(1.0).reshape(2 * SPLIT, 2, scene, local)
    left = left.transpose(0, 2, 1, 3).reshape(2 * SPLIT, 2 * SPLIT)
    phase = azimuth_phase.reshape(SPLIT, SPLIT, 2, GROUPS)
    phase = phase.transpose(3, 1, 2, 0).reshape(GROUPS, SPLIT, LANES)
    weight, cos_phase, sin_phase = make_weights(band_offset, phase)
    dop, last, initial = forward(arrived, dates, left)
    before, after = shifted(last, initial, "scene")
    looked = focus(dop, before, after, weight, cos_phase, sin_phase)
    before, after = shifted(looked[CHUNKS - HALO_CHUNKS :], looked[:HALO_CHUNKS], "scene")
    result = filtered(looked, before, after, pairs)
    return result.reshape(pairs, 2, STRIP, -1).transpose(0, 3, 1, 2)


def solution(mesh):
    return jax.shard_map(
        on_device,
        mesh=mesh,
        in_specs=(
            P("scene", None, "stack", None),
            P("stack", "scene"),
            P(("stack", "scene")),
            P("stack", None),
        ),
        out_specs=P("stack", None, None, "scene"),
        check_vma=False,
    )
```

profile of v0, /device:TPU:18, one launch (start us, length us, event | category | flops | bytes accessed | tf_op | source)
XLA Modules:
  0.0 107.5 jit_solution(3340973958685678336)
XLA Ops:
  0.0 2.4 %copy.21 = bf16[256,2,2,512]{0,3,2,1:T(8,128)(2,1)S(1)} copy(bf16[256,2,2,512]{3,2,1,0:T(2,128)(2,1)} %param.17) | data formatting | bytes 2097152 | tf_op args[0]
  2.4 0.9 reshape.18
  3.3 3.5 %copy.22 = bf16[16,2,4,2,16,2,64]{6,5,4,3,2,1,0:T(2,128)(2,1)} copy(bf16[16,2,4,2,16,2,64]{6,2,4,5,0,3,1:T(4,128)(2,1)S(1)} %bitcast.12) | data formatting | bytes 2097152 | tf_op jit(solution)/shard_map/transpose | solution.py:412
  6.8 5.3 %reshape.19 = bf16[16,8,4096]{2,1,0:T(8,128)(2,1)S(1)} reshape(bf16[16,2,4,2,16,2,64]{6,5,4,3,2,1,0:T(2,128)(2,1)} %copy.22) | data formatting | bytes 2097152 | tf_op jit(solution)/shard_map/reshape | solution.py:412
  12.1 0.0 copy-start
  12.1 31.3 %all_to_all.5 = bf16[16,8,4096]{2,1,0:T(8,128)(2,1)} all-to-all(bf16[16,8,4096]{2,1,0:T(8,128)(2,1)S(1)} %reshape.19), channel_id=1, replica_groups=mesh['stack'=2,'scene'=16] {'scene'}, dimensions={0} | all-to-all | bytes 2097152 | tf_op jit(solution)/shard_map/all_to_all | solution.py:415
  43.4 6.7 %forward.1 = (bf16[2,16,64,256]{3,2,1,0:T(8,128)(2,1)}, bf16[2,8,64,128]{3,2,1,0:T(8,128)(2,1)}, bf16[2,8,64,128]{3,2,1,0:T(8,128)(2,1)}) custom-call(bf16[128,4096]{1,0:T(8,128)(2,1)} %bitcast.13, bf16[128,128]{1,0:T(8,128)(2,1)} %constant.22.clone.left_ref, bf16[256,256]{1,0:T(8,128)(2,1)} %constant.23.clone.right_ref, f32[64,128]{1,0:T(8,128)} %constant.24.clone.tc_ref, ...), custom_call_target="tpu_custom_call" | custom-call | tf_op jit(solution)/shard_map/forward/pallas_call | solution.py:197
  50.1 1.9 %collective-permute-start = (bf16[2,8,64,128]{3,2,1,0:T(8,128)(2,1)}, bf16[2,8,64,128]{3,2,1,0:T(8,128)(2,1)S(1)}, u32[]{:S(2)}, u32[]{:S(2)}) collective-permute-start(bf16[2,8,64,128]{3,2,1,0:T(8,128)(2,1)} %get-tuple-element.12), channel_id=1, source_target_pairs={{0,1},{1,2},{2,3},{3,4},{4,5},{5,6},{6,7},{7,8},{8,9},{9,10},{10,1... | collective-permute-start | bytes 786440 | tf_op jit(solution)/shard_map/ppermute | solution.py:402
  52.0 4.5 %collective-permute-start.1 = (bf16[2,8,64,128]{3,2,1,0:T(8,128)(2,1)}, bf16[2,8,64,128]{3,2,1,0:T(8,128)(2,1)S(1)}, u32[]{:S(2)}, u32[]{:S(2)}) collective-permute-start(bf16[2,8,64,128]{3,2,1,0:T(8,128)(2,1)} %get-tuple-element.13), channel_id=1, source_target_pairs={{1,0},{2,1},{3,2},{4,3},{5,4},{6,5},{7,6},{8,7},{9,8},{10,9},{11,1... | collective-permute-start | bytes 786440 | tf_op jit(solution)/shard_map/ppermute | solution.py:402
  56.6 0.0 copy-done
  56.6 0.4 reshape.21
  57.0 0.6 copy.23
  57.6 1.4 %reshape.22.phase_ref = f32[16,64,128]{2,1,0:T(8,128)} reshape(f32[16,64,2,64]{3,2,1,0:T(2,128)S(1)} %bitcast.14) | data formatting | bytes 1048576 | tf_op jit(solution)/shard_map/reshape | solution.py:420
  59.0 12.5 %weights.1 = (f32[16,15,64,128]{3,2,1,0:T(8,128)}, f32[16,64,128]{2,1,0:T(8,128)}, f32[16,64,128]{2,1,0:T(8,128)}) custom-call(s32[32]{0:T(128)} %band_ref.1, f32[16,64,128]{2,1,0:T(8,128)} %reshape.22.phase_ref), custom_call_target="tpu_custom_call" | custom-call | flops 60000000 | bytes 10000000 | tf_op jit(solution)/shard_map/weights/pallas_call | solution.py:151
  71.6 0.0 collective-permute-done.before_ref
  71.6 0.0 copy-start.1
  71.6 0.0 collective-permute-done.1.after_ref
  71.6 0.0 copy-start.2
  71.6 0.7 copy-done.1
  72.3 0.1 copy-done.2
  72.3 15.9 %focus.1.own_ref = bf16[8,64,128]{2,1,0:T(8,128)(2,1)} custom-call(bf16[2,16,64,256]{3,2,1,0:T(8,128)(2,1)} %get-tuple-element.11.dop_ref, bf16[2,8,64,128]{3,2,1,0:T(8,128)(2,1)} %copy-done.1, bf16[2,8,64,128]{3,2,1,0:T(8,128)(2,1)} %copy-done.2, f32[16,15,64,128]{3,2,1,0:T(8,128)} %get-tuple-element.14.weight_ref, ...), custom_call_target="tpu_custom_call" | custom-call | tf_op jit(solution)/shard_map/focus/pallas_call | solution.py:291
  88.2 0.9 fusion
  89.1 1.9 %collective-permute-start.3 = (bf16[4,64,128]{2,1,0:T(8,128)(2,1)S(1)}, bf16[4,64,128]{2,1,0:T(8,128)(2,1)S(1)}, u32[]{:S(2)}, u32[]{:S(2)}) collective-permute-start(bf16[4,64,128]{2,1,0:T(8,128)(2,1)S(1)} %get-tuple-element.17), channel_id=1, source_target_pairs={{1,0},{2,1},{3,2},{4,3},{5,4},{6,5},{7,6},{8,7},{9,8},{10,9},{11,1... | collective-permute-start | bytes 196616 | tf_op jit(solution)/shard_map/ppermute | solution.py:402
  91.1 2.4 %collective-permute-start.2 = (bf16[4,64,128]{2,1,0:T(8,128)(2,1)S(1)}, bf16[4,64,128]{2,1,0:T(8,128)(2,1)S(1)}, u32[]{:S(2)}, u32[]{:S(2)}) collective-permute-start(bf16[4,64,128]{2,1,0:T(8,128)(2,1)S(1)} %get-tuple-element.18), channel_id=1, source_target_pairs={{0,1},{1,2},{2,3},{3,4},{4,5},{5,6},{6,7},{7,8},{8,9},{9,10},{10,1... | collective-permute-start | bytes 196616 | tf_op jit(solution)/shard_map/ppermute | solution.py:402
  93.5 0.0 collective-permute-done.3.after_ref
  93.5 0.0 copy-start.3
  93.5 4.0 %collective-permute-done.2.before_ref = bf16[4,64,128]{2,1,0:T(8,128)(2,1)S(1)} collective-permute-done((bf16[4,64,128]{2,1,0:T(8,128)(2,1)S(1)}, bf16[4,64,128]{2,1,0:T(8,128)(2,1)S(1)}, u32[]{:S(2)}, u32[]{:S(2)}) %collective-permute-start.2) | collective-permute-done | bytes 65568 | tf_op jit(solution)/shard_map/ppermute | solution.py:402
  97.5 0.0 copy-done.3
  97.5 0.0 copy-start.4
  97.5 0.6 copy-done.4
  98.2 9.4 %filter.1 = bf16[2,64,1024]{2,1,0:T(8,128)(2,1)} custom-call(bf16[8,64,128]{2,1,0:T(8,128)(2,1)} %focus.1.own_ref, bf16[4,64,128]{2,1,0:T(8,128)(2,1)} %copy-done.4, bf16[4,64,128]{2,1,0:T(8,128)(2,1)} %copy-done.3, bf16[512,512]{1,0:T(8,128)(2,1)} %constant.29.clone.azimuth_ref, bf16[64,128]{1,0:T(8,128)(2,1)} %constant.30.clone.range_ref, ...), custom_call_target="tpu_custom_call" | custom-call | tf_op jit(solution)/shard_map/filter/pallas_call | solution.py:380
Async XLA Ops:
  12.1 44.4 %copy-start = (f32[4096,32]{0,1:T(8,128)S(1)}, f32[4096,32]{0,1:T(8,128)}, u32[]{:S(2)}) copy-start(f32[4096,32]{0,1:T(8,128)} %param.18) | copy-start | bytes 1572868
  50.1 21.5 %collective-permute-start = (bf16[2,8,64,128]{3,2,1,0:T(8,128)(2,1)}, bf16[2,8,64,128]{3,2,1,0:T(8,128)(2,1)S(1)}, u32[]{:S(2)}, u32[]{:S(2)}) collective-permute-start(bf16[2,8,64,128]{3,2,1,0:T(8,128)(2,1)} %get-tuple-element.12), channel_id=1, source_target_pairs={{0,1},{1,2},{2,3},{3,4},{4,5},{5,6},{6,7},{7,8},{8,9},{9,10},{10,1... | collective-permute-start | bytes 786440 | tf_op jit(solution)/shard_map/ppermute | solution.py:402
  52.0 19.6 %collective-permute-start.1 = (bf16[2,8,64,128]{3,2,1,0:T(8,128)(2,1)}, bf16[2,8,64,128]{3,2,1,0:T(8,128)(2,1)S(1)}, u32[]{:S(2)}, u32[]{:S(2)}) collective-permute-start(bf16[2,8,64,128]{3,2,1,0:T(8,128)(2,1)} %get-tuple-element.13), channel_id=1, source_target_pairs={{1,0},{2,1},{3,2},{4,3},{5,4},{6,5},{7,6},{8,7},{9,8},{10,9},{11,1... | collective-permute-start | bytes 786440 | tf_op jit(solution)/shard_map/ppermute | solution.py:402
  71.6 0.7 copy-start.1
  71.6 0.8 copy-start.2
  89.1 4.3 %collective-permute-start.3 = (bf16[4,64,128]{2,1,0:T(8,128)(2,1)S(1)}, bf16[4,64,128]{2,1,0:T(8,128)(2,1)S(1)}, u32[]{:S(2)}, u32[]{:S(2)}) collective-permute-start(bf16[4,64,128]{2,1,0:T(8,128)(2,1)S(1)} %get-tuple-element.17), channel_id=1, source_target_pairs={{1,0},{2,1},{3,2},{4,3},{5,4},{6,5},{7,6},{8,7},{9,8},{10,9},{11,1... | collective-permute-start | bytes 196616 | tf_op jit(solution)/shard_map/ppermute | solution.py:402
  91.1 6.5 %collective-permute-start.2 = (bf16[4,64,128]{2,1,0:T(8,128)(2,1)S(1)}, bf16[4,64,128]{2,1,0:T(8,128)(2,1)S(1)}, u32[]{:S(2)}, u32[]{:S(2)}) collective-permute-start(bf16[4,64,128]{2,1,0:T(8,128)(2,1)S(1)} %get-tuple-element.18), channel_id=1, source_target_pairs={{0,1},{1,2},{2,3},{3,4},{4,5},{5,6},{6,7},{7,8},{8,9},{9,10},{10,1... | collective-permute-start | bytes 196616 | tf_op jit(solution)/shard_map/ppermute | solution.py:402
  93.5 4.1 %copy-start.3 = (bf16[4,64,128]{2,1,0:T(8,128)(2,1)}, bf16[4,64,128]{2,1,0:T(8,128)(2,1)S(1)}, u32[]{:S(2)}) copy-start(bf16[4,64,128]{2,1,0:T(8,128)(2,1)S(1)} %collective-permute-done.3.after_ref) | copy-start | bytes 196612
  97.5 0.6 copy-start.4
where the time goes:
time: 109 us; the launch traced here: 108 us
  Pallas kernels  44.5 us (41%)
  blocking collectives  31.3 us (29%)
  local copies, waits for them, and re-layouts  16.8 us (15%)
  starting transfers between devices  10.8 us (10%)
  waiting for transfers between devices  4.06 us (4%)
    all_to_all x1, blocking collectives, on_device(): lax.all_to_all(pieces, 'scene', split_axis=0, concat_axis=0, tiled=True)  31.3 us
    pallas_call x1, Pallas kernels, focus(): pl.pallas_call(focus_kernel, in_specs=whole(11), out_specs=pl.BlockSpec(m...  15.9 us
    pallas_call x1, Pallas kernels, make_weights(): pl.pallas_call(weights_kernel, grid=(GROUPS,), in_specs=[pl.BlockSpec(mem...  12.5 us
    ppermute x4, starting transfers between devices, shifted(): return (lax.ppermute(last, axis, up), lax.ppermute(initial, axis, down))  10.8 us
    pallas_call x1, Pallas kernels, filtered(): pl.pallas_call(filter_kernel, in_specs=whole(7), out_specs=pl.BlockSpec(m...  9.37 us
    pallas_call x1, Pallas kernels, forward(): pl.pallas_call(forward_kernel, in_specs=whole(5), out_specs=whole(3), out...  6.66 us
    reshape x1, local copies, waits for them, and re-layouts, on_device(): pieces.transpose(4, 2, 0, 3, 6, 5, 1)  5.29 us
    ppermute x4, waiting for transfers between devices, shifted(): return (lax.ppermute(last, axis, up), lax.ppermute(initial, axis, down))  4.06 us
  transfers between devices with their start and end apart: 4, of which 1 were waited for; matrix products, arithmetic and copies ran while one was open for 2% of the time, Pallas kernels for 12%

commit v1 on v0

v1 whole, which is shorter than its diff:
```python
import math

import jax
import jax.numpy as jnp
import numpy as np
from jax import lax
from jax.experimental import pallas as pl
from jax.experimental.pallas import tpu as pltpu
from jax.sharding import PartitionSpec as P

SPLIT = 64
LOOKS = 4
PATCH = 64
SHIFT = 8
TAPS = 2 * SHIFT - 1
EPSILON = 1e-06
STRIP = 32
GROUPS = STRIP // 2
LANES = 2 * SPLIT
CHUNKS = STRIP // 4
HALO_CHUNKS = CHUNKS // 2
VMEM_LIMIT = 56 * 1024 * 1024


def base_tables():
    k = np.arange(64)
    angle = 2.0 * np.pi * ((k[:, None] * k[None, :]) % 64) / 64.0
    return np.cos(angle), np.sin(angle)


def twiddle_tables():
    k = np.arange(SPLIT)
    angle = 2.0 * np.pi * ((k[:, None] * k[None, :]) % (SPLIT * SPLIT)) / (SPLIT * SPLIT)
    return (
        np.tile(np.cos(angle), (1, 2)).astype(np.float32),
        np.tile(np.sin(angle), (1, 2)).astype(np.float32),
    )


def bf16(table):
    return jnp.asarray(np.asarray(table, np.float32), jnp.bfloat16)


def left_table(direction):
    c, s = base_tables()
    return np.block([[c, direction * s], [-direction * s, c]])


def right_table(direction):
    c, s = base_tables()
    eye = np.eye(2)
    return np.block(
        [
            [np.kron(eye, c), np.kron(eye, -direction * s)],
            [np.kron(eye, direction * s), np.kron(eye, c)],
        ]
    )


def look_table():
    table = np.zeros((4, 2, 2, SPLIT, 2, 4, 2, SPLIT // LOOKS))
    for g in range(4):
        for c in range(2):
            for rb in range(2):
                for q in range(SPLIT):
                    table[g, c, rb, q, rb, g, c, q // LOOKS] = 1.0 / LOOKS
    return table.reshape(4 * 2 * 2 * SPLIT, 2 * 4 * 2 * SPLIT // LOOKS)


def patch_azimuth_table():
    c, s = base_tables()
    table = np.zeros((4, 4, 2, 16, 4, 2, 64))
    for p in range(4):
        part_c, part_s = c[16 * p : 16 * p + 16], s[16 * p : 16 * p + 16]
        for r in range(4):
            table[p, r, 0, :, r, 0] = part_c
            table[p, r, 1, :, r, 0] = part_s
            table[p, r, 0, :, r, 1] = -part_s
            table[p, r, 1, :, r, 1] = part_c
    return table.reshape(512, 512)


def patch_range_table():
    c, s = base_tables()
    return np.concatenate([c, s], axis=1)


def back_azimuth_table():
    c, s = base_tables()
    c, s = c[:, 16:48], s[:, 16:48]
    table = np.zeros((4, 2, 64, 2, 4, 32))
    for i in range(4):
        table[i, 0, :, 0, i] = c
        table[i, 1, :, 0, i] = -s
        table[i, 0, :, 1, i] = s
        table[i, 1, :, 1, i] = c
    return table.reshape(512, 256)


def back_range_table():
    c, s = base_tables()
    c, s = c[16:48], s[16:48]
    return np.block([[c, -s], [s, c]])


def dot(a, b):
    return jnp.dot(a, b, preferred_element_type=jnp.float32)


def lane_order():
    lane = np.arange(SPLIT)
    return 2 * (lane % (SPLIT // 2)) + lane // (SPLIT // 2)


def spectrum_side(table, axis):
    order = np.concatenate([SPLIT * half + lane_order() for half in range(4)])
    return np.take(table, order, axis=axis)


def make_weights(g, band_ref, phase_ref, weight_ref, cos_ref, sin_ref):
    shape = (SPLIT, LANES)
    lane = lax.broadcasted_iota(jnp.int32, shape, 1)
    row = lax.broadcasted_iota(jnp.int32, shape, 0)
    half = SPLIT // 2
    k = row + SPLIT * (2 * (lane & (half - 1)) + ((lane & half) // half))
    total = SPLIT * SPLIT
    f = jnp.where(k < total // 2, k, k - total).astype(jnp.float32)
    ratio = f * (2.0 / total)
    band = jnp.where(lane < SPLIT, band_ref[g], band_ref[g + GROUPS]).astype(jnp.float32)
    s = band * (ratio * ratio - 0.5)
    n = jnp.floor(s + 0.5)
    y = s - n
    y2 = y * y
    pi = math.pi
    poly = -(pi**11) / 39916800.0
    for power, fact in ((9, 362880.0), (7, -5040.0), (5, 120.0), (3, -6.0), (1, 1.0)):
        poly = poly * y2 + (pi**power) / fact
    odd = n.astype(jnp.int32) & 1
    lobe = jnp.where(odd == 1, 1.0, -1.0) * (y * poly) * (1.0 / pi)
    cos_s = 0.5 * jnp.cos(s * (pi / 4.0))
    sin_s = 0.5 * jnp.sin(s * (pi / 4.0))
    for tap in range(TAPS):
        m = tap + 1 - SHIFT
        x = m - s
        sign = 1.0 if m % 2 == 0 else -1.0
        safe = jnp.where(x == 0.0, 1.0, x)
        sinc = jnp.where(x == 0.0, 1.0, (sign * lobe) / safe)
        window = 0.5 + math.cos(pi * m / 4.0) * cos_s + math.sin(pi * m / 4.0) * sin_s
        weight_ref[g, tap] = jnp.where(jnp.abs(x) < SHIFT / 2.0, sinc * window, 0.0)
    first, second = phase_ref[g], phase_ref[g + GROUPS]
    pieces = [first, pltpu.roll(first, SPLIT, 1), second, pltpu.roll(second, SPLIT, 1)]
    angle = jnp.concatenate(pieces, axis=0).T[:SPLIT]
    cos_ref[g] = jnp.cos(angle)
    sin_ref[g] = jnp.sin(angle)


def arrived_lines(wide_ref, g, sources, local, low):
    rows = []
    for c in range(2):
        for pair in range(wide_ref.shape[1]):
            one = wide_ref[c, pair, pl.ds(g, sources, stride=STRIP)]
            two = wide_ref[c, pair, pl.ds(g + GROUPS, sources, stride=STRIP)]
            rows.append(jnp.where(low[:sources], one, pltpu.roll(two, SPLIT, 1)))
            if local > 1:
                rows.append(jnp.where(low[:sources], pltpu.roll(one, SPLIT, 1), two))
    return jnp.concatenate(rows, axis=0).astype(jnp.bfloat16)


def scene_kernel(
    raw_ref, band_ref, phase_ref,
    left_ref, right_ref, back_right_ref, back_left_ref, tc_ref, ts_ref, look_ref,
    azimuth_ref, range_ref, back_azimuth_ref, back_range_ref,
    out_ref,
    recv_ref, wide_ref, weight_ref, cos_ref, sin_ref, ext_ref,
    up_ref, down_ref, before_ref, after_ref, high_ref, low_ref,
    own_ref, own_before_ref, own_after_ref, line_ref, grid_ref,
    send_sem, recv_sem, local_sem, edge_send, edge_recv, look_send, look_recv,
):
    scene = lax.axis_size("scene")
    me = lax.axis_index("scene")
    dates = raw_ref.shape[1]
    local = raw_ref.shape[3] // SPLIT
    low = lax.broadcasted_iota(jnp.int32, (SPLIT, LANES), 1) < SPLIT
    patches = SPLIT // 2

    barrier = pltpu.get_barrier_semaphore()

    def greet(o, carry):
        pl.semaphore_signal(
            barrier, inc=1, device_id={"scene": lax.rem(me + o, scene)},
            device_id_type=pl.DeviceIdType.MESH,
        )
        return carry

    lax.fori_loop(1, scene, greet, 0)
    pl.semaphore_wait(barrier, scene - 1)

    def strip_copy(d, o):
        peer = lax.rem(me + o, scene)
        start = pl.multiple_of(peer * STRIP, STRIP)
        return pltpu.make_async_remote_copy(
            src_ref=raw_ref.at[:, d, pl.ds(start, STRIP)],
            dst_ref=recv_ref.at[d, me],
            send_sem=send_sem.at[d, o],
            recv_sem=recv_sem.at[d, o],
            device_id={"scene": peer},
            device_id_type=pl.DeviceIdType.MESH,
        )

    def own_copy(d):
        start = pl.multiple_of(me * STRIP, STRIP)
        return pltpu.make_async_copy(
            raw_ref.at[:, d, pl.ds(start, STRIP)], recv_ref.at[d, me], local_sem.at[d]
        )

    for d in range(dates):

        def send(o, carry):
            strip_copy(d, o).start()
            return carry

        lax.fori_loop(1, scene, send, 0)
        own_copy(d).start()

    def weigh(g, carry):
        make_weights(g, band_ref, phase_ref, weight_ref, cos_ref, sin_ref)
        return carry

    lax.fori_loop(0, GROUPS, weigh, 0)

    @pl.when(me == 0)
    def _():
        before_ref[...] = jnp.zeros(before_ref.shape, before_ref.dtype)
        own_before_ref[...] = jnp.zeros(own_before_ref.shape, own_before_ref.dtype)

    @pl.when(me == scene - 1)
    def _():
        after_ref[...] = jnp.zeros(after_ref.shape, after_ref.dtype)
        own_after_ref[...] = jnp.zeros(own_after_ref.shape, own_after_ref.dtype)

    line_ref[...] = jnp.zeros(line_ref.shape, jnp.float32)

    def neighbour(source, target, send, recv, step):
        return pltpu.make_async_remote_copy(
            src_ref=source, dst_ref=target, send_sem=send, recv_sem=recv,
            device_id={"scene": me + step}, device_id_type=pl.DeviceIdType.MESH,
        )

    def edge_copies(d):
        return (
            neighbour(up_ref.at[d], before_ref.at[d], edge_send.at[d, 0], edge_recv.at[d, 0], 1),
            neighbour(down_ref.at[d], after_ref.at[d], edge_send.at[d, 1], edge_recv.at[d, 1], -1),
        )

    def look_copies():
        return (
            neighbour(
                own_ref.at[pl.ds(CHUNKS - HALO_CHUNKS, HALO_CHUNKS)], own_before_ref,
                look_send.at[0], look_recv.at[0], 1,
            ),
            neighbour(
                own_ref.at[pl.ds(0, HALO_CHUNKS)], own_after_ref,
                look_send.at[1], look_recv.at[1], -1,
            ),
        )

    def start_pair(copies):
        @pl.when(me < scene - 1)
        def _():
            copies[0].start()

        @pl.when(me > 0)
        def _():
            copies[1].start()

    def wait_pair(copies):
        @pl.when(me > 0)
        def _():
            copies[0].wait_recv()
            copies[1].wait_send()

        @pl.when(me < scene - 1)
        def _():
            copies[1].wait_recv()
            copies[0].wait_send()

    for d in range(dates):

        def arrive(o, carry):
            strip_copy(d, o).wait_recv()
            return carry

        lax.fori_loop(1, scene, arrive, 0)
        own_copy(d).wait()

        def widen(source, carry):
            start = pl.multiple_of(source * STRIP, STRIP)
            for c in range(2):
                strip = recv_ref[d, source, c].astype(jnp.float32)
                for pair in range(wide_ref.shape[1]):
                    part = strip[:, pair * LANES : (pair + 1) * LANES]
                    wide_ref[c, pair, pl.ds(start, STRIP), : part.shape[1]] = part
            return carry

        lax.fori_loop(0, scene, widen, 0)

        def forward(i, carry):
            for half in range(2):
                g = i + half * (GROUPS // 2)
                lines = arrived_lines(wide_ref, g, scene, local, low)
                first = dot(left_ref[...], lines)
                re, im = first[:SPLIT], first[SPLIT:]
                tc, ts = tc_ref[...], ts_ref[...]
                segment = jnp.concatenate([re * tc + im * ts, im * tc - re * ts], axis=1)
                second = dot(segment.astype(jnp.bfloat16), right_ref[...]) * (1.0 / SPLIT)
                second = second.astype(jnp.bfloat16).astype(jnp.float32)
                re, im = second[:, :LANES], second[:, LANES:]
                re_turned, im_turned = pltpu.roll(re, SPLIT, 1), pltpu.roll(im, SPLIT, 1)
                other = i + (0 if half else 3 * SHIFT)
                ext_ref[d, 0, g + SHIFT] = re
                ext_ref[d, 1, g + SHIFT] = im
                ext_ref[d, 0, other] = re_turned
                ext_ref[d, 1, other] = im_turned
                if half == 0:
                    down_ref[d, i] = jnp.where(low, re, im_turned).astype(jnp.bfloat16)
                else:
                    up_ref[d, i] = jnp.where(low, re_turned, im).astype(jnp.bfloat16)
            return carry

        lax.fori_loop(0, GROUPS // 2, forward, 0, unroll=2)
        start_pair(edge_copies(d))

    for d in range(dates):
        wait_pair(edge_copies(d))

        def fill(i, carry):
            before = before_ref[d, i].astype(jnp.float32)
            after = after_ref[d, i].astype(jnp.float32)
            before_parts = (before, pltpu.roll(before, SPLIT, 1))
            after_parts = (pltpu.roll(after, SPLIT, 1), after)
            for c in range(2):
                ext_ref[d, c, i] = jnp.where(low, before_parts[c], ext_ref[d, c, i])
                last = i + 3 * SHIFT
                ext_ref[d, c, last] = jnp.where(low, ext_ref[d, c, last], after_parts[c])
            return carry

        lax.fori_loop(0, SHIFT, fill, 0)

    def focus(g, carry):
        parts = []
        for half in range(2):
            rows = pl.ds(half * (SPLIT // 2), SPLIT // 2)
            sums = [jnp.zeros((SPLIT // 2, LANES), jnp.float32) for _ in range(2 * dates)]
            for tap in range(TAPS):
                weight = weight_ref[g, tap, rows]
                for d in range(dates):
                    for c in range(2):
                        sums[2 * d + c] += weight * ext_ref[d, c, g + tap + 1, rows]
            cos_phase, sin_phase = cos_ref[g, rows], sin_ref[g, rows]
            parts.append(
                [
                    jnp.concatenate(
                        [
                            sums[2 * d] * cos_phase - sums[2 * d + 1] * sin_phase,
                            sums[2 * d + 1] * cos_phase + sums[2 * d] * sin_phase,
                        ],
                        axis=1,
                    ).astype(jnp.bfloat16)
                    for d in range(dates)
                ]
            )
        focused = []
        for d in range(dates):
            compressed = jnp.concatenate([parts[0][d], parts[1][d]], axis=0)
            first = dot(compressed, back_right_ref[...])
            re, im = first[:, :LANES], first[:, LANES:]
            tc, ts = tc_ref[...], ts_ref[...]
            segment = jnp.concatenate([re * tc - im * ts, im * tc + re * ts], axis=0)
            second = dot(back_left_ref[...], segment.astype(jnp.bfloat16)) * (1.0 / SPLIT)
            second = second.astype(jnp.bfloat16).astype(jnp.float32)
            focused.append((second[:SPLIT], second[SPLIT:]))
        (tr, ti), (lr, li) = focused
        product = jnp.concatenate([lr * tr + li * ti, li * tr - lr * ti], axis=1)
        high = product.astype(jnp.bfloat16)
        high_ref[g] = high
        low_ref[g] = (product - high.astype(jnp.float32)).astype(jnp.bfloat16)
        return carry

    lax.fori_loop(0, GROUPS, focus, 0)
    for big in range(GROUPS // 4):
        high = jnp.concatenate([high_ref[4 * big + j] for j in range(4)], axis=1)
        rest = jnp.concatenate([low_ref[4 * big + j] for j in range(4)], axis=1)
        looked = dot(high, look_ref[...]) + dot(rest, look_ref[...])
        own_ref[big] = looked[:, :LANES].astype(jnp.bfloat16)
        own_ref[HALO_CHUNKS + big] = looked[:, LANES:].astype(jnp.bfloat16)
    start_pair(look_copies())

    def lines_of(first_chunk, count):
        def forward_lines(step, carry):
            rows = []
            for j in range(4):
                chunk = first_chunk + 4 * step + j
                rows.append(
                    jnp.concatenate(
                        [line_ref[chunk, pl.ds(p, patches, stride=2)] for p in range(4)], axis=1
                    )
                )
            lines = jnp.concatenate(rows, axis=0).astype(jnp.bfloat16)
            result = dot(lines, azimuth_ref[...]).astype(jnp.bfloat16).astype(jnp.float32)
            for j in range(4):
                for r in range(4):
                    start = ((first_chunk + 4 * step + j) * 4 + r) * patches
                    grid_ref[pl.ds(pl.multiple_of(start, patches), patches)] = result[
                        j * patches : (j + 1) * patches, r * LANES : (r + 1) * LANES
                    ]
            return carry

        lax.fori_loop(0, count // 4, forward_lines, 0)

    for j in range(CHUNKS):
        line_ref[HALO_CHUNKS + j, pl.ds(1, SPLIT)] = own_ref[j].astype(jnp.float32)
    lines_of(HALO_CHUNKS, CHUNKS)
    wait_pair(look_copies())
    for j in range(HALO_CHUNKS):
        line_ref[j, pl.ds(1, SPLIT)] = own_before_ref[j].astype(jnp.float32)
        line_ref[HALO_CHUNKS + CHUNKS + j, pl.ds(1, SPLIT)] = own_after_ref[j].astype(jnp.float32)
    lines_of(0, HALO_CHUNKS)
    lines_of(HALO_CHUNKS + CHUNKS, HALO_CHUNKS)
    sign = jnp.where(low, 1.0, -1.0)

    def filter_patches(step, carry):
        tiles = []
        for j in range(4):
            tile = grid_ref[pl.ds(4 * step + j, PATCH, stride=patches)]
            swapped = pltpu.roll(tile, PATCH, 1) * sign
            tiles.append(jnp.concatenate([tile, swapped], axis=0).astype(jnp.bfloat16))
        spectra = dot(range_ref[...], jnp.concatenate(tiles, axis=1)) * (1.0 / PATCH)
        kept = []
        for j in range(4):
            spectrum = spectra[:, j * LANES : (j + 1) * LANES]
            power = spectrum * spectrum
            magnitude = jnp.sqrt(power + pltpu.roll(power, PATCH, 1) + EPSILON)
            row_sum = (
                magnitude
                + pltpu.roll(magnitude, 1, 0)
                + pltpu.roll(magnitude, PATCH - 1, 0)
            )
            smooth = (row_sum + pltpu.roll(row_sum, 1, 1) + pltpu.roll(row_sum, LANES - 1, 1)) * (
                1.0 / 9.0
            )
            level = jnp.sum(jnp.sum(magnitude, axis=0, keepdims=True), axis=1, keepdims=True)
            level = level * (1.0 / (PATCH * LANES)) + EPSILON
            kept.append((spectrum * (smooth / level)).astype(jnp.bfloat16))
        back = dot(jnp.concatenate(kept, axis=1), back_azimuth_ref[...]).astype(jnp.bfloat16)
        stacked = jnp.concatenate([back[:, :LANES], back[:, LANES:]], axis=0)
        result = (dot(back_range_ref[...], stacked) * (1.0 / PATCH)).astype(jnp.bfloat16)
        start = pl.multiple_of(step * LANES, LANES)
        for pair in range(out_ref.shape[0]):
            out_ref[pair, :, pl.ds(start, LANES)] = result
        return carry

    lax.fori_loop(0, patches // 4, filter_patches, 0)

    for d in range(dates):

        def sent(o, carry):
            strip_copy(d, o).wait_send()
            return carry

        lax.fori_loop(1, scene, sent, 0)


def run_scene(raw, band, phase, left, scene, pairs):
    dates = raw.shape[1]
    width = raw.shape[3]
    looks = SPLIT * SPLIT // LOOKS
    tc, ts = twiddle_tables()
    vmem = pl.BlockSpec(memory_space=pltpu.VMEM)
    plane = (GROUPS, SPLIT, LANES)
    edge = pltpu.VMEM((dates, SHIFT, SPLIT, LANES), jnp.bfloat16)
    looked_edge = pltpu.VMEM((HALO_CHUNKS, SPLIT, LANES), jnp.bfloat16)
    products = pltpu.VMEM((GROUPS, SPLIT, 2 * LANES), jnp.bfloat16)
    dma = pltpu.SemaphoreType.DMA
    return pl.pallas_call(
        scene_kernel,
        in_specs=[pl.BlockSpec(memory_space=pl.ANY), pl.BlockSpec(memory_space=pltpu.SMEM)]
        + [vmem] * 12,
        out_specs=vmem,
        out_shape=jax.ShapeDtypeStruct((pairs, 2 * STRIP, looks), jnp.bfloat16),
        scratch_shapes=[
            pltpu.VMEM((dates, scene, 2, STRIP, width), jnp.bfloat16),
            pltpu.VMEM((2, pl.cdiv(width, LANES), scene * STRIP, LANES), jnp.float32),
            pltpu.VMEM((GROUPS, TAPS, SPLIT, LANES), jnp.float32),
            pltpu.VMEM(plane, jnp.float32),
            pltpu.VMEM(plane, jnp.float32),
            pltpu.VMEM((dates, 2, GROUPS + 2 * SHIFT, SPLIT, LANES), jnp.float32),
            edge, edge, edge, edge, products, products,
            pltpu.VMEM((CHUNKS, SPLIT, LANES), jnp.bfloat16),
            looked_edge,
            looked_edge,
            pltpu.VMEM((2 * CHUNKS, SPLIT + 8, LANES), jnp.float32),
            pltpu.VMEM((PATCH * SPLIT // 2, LANES), jnp.float32),
            dma((dates, scene)), dma((dates, scene)), dma((dates,)),
            dma((dates, 2)), dma((dates, 2)), dma((2,)), dma((2,)),
        ],
        compiler_params=pltpu.CompilerParams(
            vmem_limit_bytes=VMEM_LIMIT, collective_id=0, has_side_effects=True
        ),
        name="scene",
    )(
        raw, band, phase, bf16(left), bf16(spectrum_side(right_table(1.0), 1)),
        bf16(spectrum_side(right_table(-1.0), 0)), bf16(left_table(-1.0)),
        jnp.asarray(tc), jnp.asarray(ts), bf16(look_table()),
        bf16(patch_azimuth_table()), bf16(patch_range_table()),
        bf16(back_azimuth_table()), bf16(back_range_table()),
    )


def on_device(raw_echoes, azimuth_phase, band_offset, partners):
    scene = lax.axis_size("scene")
    dates = raw_echoes.shape[2]
    local = raw_echoes.shape[0] // SPLIT
    pairs = partners.size
    assert dates == 2 and raw_echoes.shape[3] == scene * STRIP
    left = left_table(1.0).reshape(2 * SPLIT, 2, scene, local)
    left = left.transpose(0, 1, 3, 2).reshape(2 * SPLIT, 2 * SPLIT)
    raw = raw_echoes.transpose(1, 2, 3, 0)
    phase = azimuth_phase.T.reshape(STRIP, SPLIT // 2, LANES)
    result = run_scene(raw, band_offset, phase, left, scene, pairs)
    return result.reshape(pairs, 2, STRIP, -1).transpose(0, 3, 1, 2)


def solution(mesh):
    return jax.shard_map(
        on_device,
        mesh=mesh,
        in_specs=(
            P("scene", None, "stack", None),
            P("stack", "scene"),
            P(("stack", "scene")),
            P("stack", None),
        ),
        out_specs=P("stack", None, None, "scene"),
        check_vma=False,
    )
```

time: 109 us -> 64.3 us (0.59)
  the two profiles are of different devices: /device:TPU:18 before, /device:TPU:13 now
where the time goes in v1:
time: 64.3 us; the launch traced here: 64.1 us
  Pallas kernels  58.2 us (91%)
  local copies, waits for them, and re-layouts  5.9 us (9%)
    pallas_call x1, Pallas kernels, run_scene(): pl.pallas_call(scene_kernel, in_specs=[pl.BlockSpec(memory_space=pl.ANY),...  58.2 us
    unnamed x5, local copies, waits for them, and re-layouts  5.9 us

profile of v1, /device:TPU:13, one launch (start us, length us, event | category | flops | bytes accessed | tf_op | source)
XLA Modules:
  0.0 64.1 jit_solution(3762826774609885554)
XLA Ops:
  0.0 0.0 copy-start
  0.0 2.0 %copy.16 = f32[4,8,32,128]{3,2,1,0:T(8,128)} copy(f32[4,8,32,128]{3,1,2,0:T(8,128)} %bitcast.10) | data formatting | bytes 1048576
  2.0 0.0 copy-done
  2.0 2.2 %copy.15 = bf16[256,2,2,512]{0,3,2,1:T(8,128)(2,1)} copy(bf16[256,2,2,512]{3,2,1,0:T(2,128)(2,1)S(1)} %copy-done) | data formatting | bytes 2097152 | tf_op args[0]
  4.2 58.2 %scene.1 = bf16[2,64,1024]{2,1,0:T(8,128)(2,1)} custom-call(bf16[2,2,512,256]{3,2,1,0:T(8,128)(2,1)} %bitcast.7, s32[32]{0:T(128)} %band_ref.1, f32[32,32,128]{2,1,0:T(8,128)} %bitcast.8, bf16[128,128]{1,0:T(8,128)(2,1)} %constant.22.clone.left_ref, bf16[256,256]{1,0:T(8,128)(2,1)} %constant.23.clone.right_ref, ...), custom_call_target="tpu_custom_call" | custom-call | tf_op jit(solution)/shard_map/scene/pallas_call | solution.py:484
  62.4 1.7 %copy.18 = bf16[2,1024,2,32]{1,3,2,0:T(8,128)(2,1)} copy(bf16[2,1024,2,32]{1,3,2,0:T(8,128)(2,1)} %bitcast.9) | data formatting | bytes 524288
Async XLA Ops:
  0.0 2.0 %copy-start = (bf16[256,2,2,512]{3,2,1,0:T(2,128)(2,1)S(1)}, bf16[256,2,2,512]{3,2,1,0:T(2,128)(2,1)}, u32[]{:S(2)}) copy-start(bf16[256,2,2,512]{3,2,1,0:T(2,128)(2,1)} %param.15) | copy-start | bytes 3145732

commit v2 on v1

--- a/solution.py
+++ b/solution.py
@@ -19,6 +19,7 @@
 LANES = 2 * SPLIT
 CHUNKS = STRIP // 4
 HALO_CHUNKS = CHUNKS // 2
+TABLES = 13
 VMEM_LIMIT = 56 * 1024 * 1024
 
 
@@ -117,7 +118,20 @@
     return np.take(table, order, axis=axis)
 
 
-def make_weights(g, band_ref, phase_ref, weight_ref, cos_ref, sin_ref):
+def cos_sin(angle):
+    h = 0.5 * angle
+    h2 = h * h
+    sin_h = 1.0 / 6227020800.0
+    for fact in (-39916800.0, 362880.0, -5040.0, 120.0, -6.0, 1.0):
+        sin_h = sin_h * h2 + 1.0 / fact
+    sin_h = sin_h * h
+    cos_h = 1.0 / 479001600.0
+    for fact in (-3628800.0, 40320.0, -720.0, 24.0, -2.0, 1.0):
+        cos_h = cos_h * h2 + 1.0 / fact
+    return 1.0 - 2.0 * sin_h * sin_h, 2.0 * sin_h * cos_h
+
+
+def make_weights(g, band_ref, lines_ref, weight_ref, cos_ref, sin_ref):
     shape = (SPLIT, LANES)
     lane = lax.broadcasted_iota(jnp.int32, shape, 1)
     row = lax.broadcasted_iota(jnp.int32, shape, 0)
@@ -137,8 +151,8 @@
         poly = poly * y2 + (pi**power) / fact
     odd = n.astype(jnp.int32) & 1
     lobe = jnp.where(odd == 1, 1.0, -1.0) * (y * poly) * (1.0 / pi)
-    cos_s = 0.5 * jnp.cos(s * (pi / 4.0))
-    sin_s = 0.5 * jnp.sin(s * (pi / 4.0))
+    cos_s, sin_s = cos_sin(s * (pi / 4.0))
+    cos_s, sin_s = 0.5 * cos_s, 0.5 * sin_s
     for tap in range(TAPS):
         m = tap + 1 - SHIFT
         x = m - s
@@ -147,11 +161,11 @@
         sinc = jnp.where(x == 0.0, 1.0, (sign * lobe) / safe)
         window = 0.5 + math.cos(pi * m / 4.0) * cos_s + math.sin(pi * m / 4.0) * sin_s
         weight_ref[g, tap] = jnp.where(jnp.abs(x) < SHIFT / 2.0, sinc * window, 0.0)
-    first, second = phase_ref[g], phase_ref[g + GROUPS]
+    first = lines_ref[pl.ds(g, SPLIT // 2, stride=STRIP)]
+    second = lines_ref[pl.ds(g + GROUPS, SPLIT // 2, stride=STRIP)]
     pieces = [first, pltpu.roll(first, SPLIT, 1), second, pltpu.roll(second, SPLIT, 1)]
     angle = jnp.concatenate(pieces, axis=0).T[:SPLIT]
-    cos_ref[g] = jnp.cos(angle)
-    sin_ref[g] = jnp.sin(angle)
+    cos_ref[g], sin_ref[g] = cos_sin(angle)
 
 
 def arrived_lines(wide_ref, g, sources, local, low):
@@ -167,14 +181,15 @@
 
 
 def scene_kernel(
-    raw_ref, band_ref, phase_ref,
+    band_ref, packed_ref, phase_ref,
     left_ref, right_ref, back_right_ref, back_left_ref, tc_ref, ts_ref, look_ref,
     azimuth_ref, range_ref, back_azimuth_ref, back_range_ref,
     out_ref,
-    recv_ref, wide_ref, weight_ref, cos_ref, sin_ref, ext_ref,
-    up_ref, down_ref, before_ref, after_ref, high_ref, low_ref,
+    raw_ref, spread_ref, recv_ref, lines_ref, wide_ref, weight_ref, cos_ref, sin_ref, ext_ref,
+    up_ref, down_ref, before_ref, after_ref, focused_ref, high_ref, low_ref,
     own_ref, own_before_ref, own_after_ref, line_ref, grid_ref,
     send_sem, recv_sem, local_sem, edge_send, edge_recv, look_send, look_recv,
+    loads,
 ):
     scene = lax.axis_size("scene")
     me = lax.axis_index("scene")
@@ -193,6 +208,33 @@
         return carry
 
     lax.fori_loop(1, scene, greet, 0)
+    for load in loads:
+        load.start()
+    loads[0].wait()
+    height = packed_ref.shape[0]
+    piece = height // 8
+
+    def spread(i, carry):
+        rows = pl.ds(pl.multiple_of(i * piece, piece), piece)
+        spread_ref[rows] = packed_ref[rows].astype(jnp.float32)
+        return carry
+
+    lax.fori_loop(0, 8, spread, 0)
+    tiles = raw_ref.shape[2] // LANES
+    stride = 2 * tiles * dates
+
+    def turn(d):
+        def body(tile, carry):
+            for c in range(2):
+                start = (c * tiles + tile) * dates + d
+                lines = spread_ref[pl.ds(start, raw_ref.shape[3], stride=stride)]
+                target = pl.ds(pl.multiple_of(tile * LANES, LANES), LANES)
+                raw_ref[c, d, target] = lines.T.astype(jnp.bfloat16)
+            return carry
+
+        lax.fori_loop(0, tiles, body, 0)
+
+    turn(0)
     pl.semaphore_wait(barrier, scene - 1)
 
     def strip_copy(d, o):
@@ -213,17 +255,27 @@
             raw_ref.at[:, d, pl.ds(start, STRIP)], recv_ref.at[d, me], local_sem.at[d]
         )
 
+    held = scene - scene // 3
+
     for d in range(dates):
 
         def send(o, carry):
             strip_copy(d, o).start()
             return carry
 
-        lax.fori_loop(1, scene, send, 0)
+        if d:
+            turn(d)
+        lax.fori_loop(1, held if d else scene, send, 0)
         own_copy(d).start()
 
+    for load in loads[1:]:
+        load.wait()
+
+    for part in range(SPLIT // 2):
+        lines_ref[pl.ds(part * STRIP, STRIP)] = phase_ref[:, part * LANES : (part + 1) * LANES]
+
     def weigh(g, carry):
-        make_weights(g, band_ref, phase_ref, weight_ref, cos_ref, sin_ref)
+        make_weights(g, band_ref, lines_ref, weight_ref, cos_ref, sin_ref)
         return carry
 
     lax.fori_loop(0, GROUPS, weigh, 0)
@@ -283,6 +335,54 @@
         def _():
             copies[1].wait_recv()
             copies[0].wait_send()
+
+    def focus_date(d):
+        wait_pair(edge_copies(d))
+
+        def fill(i, carry):
+            before = before_ref[d, i].astype(jnp.float32)
+            after = after_ref[d, i].astype(jnp.float32)
+            before_parts = (before, pltpu.roll(before, SPLIT, 1))
+            after_parts = (pltpu.roll(after, SPLIT, 1), after)
+            for c in range(2):
+                ext_ref[d, c, i] = jnp.where(low, before_parts[c], ext_ref[d, c, i])
+                last = i + 3 * SHIFT
+                ext_ref[d, c, last] = jnp.where(low, ext_ref[d, c, last], after_parts[c])
+            return carry
+
+        lax.fori_loop(0, SHIFT, fill, 0, unroll=2)
+
+        def focus(g, carry):
+            re_sum = jnp.zeros((SPLIT, LANES), jnp.float32)
+            im_sum = jnp.zeros((SPLIT, LANES), jnp.float32)
+            for tap in range(TAPS):
+                weight = weight_ref[g, tap]
+                re_sum += weight * ext_ref[d, 0, g + tap + 1]
+                im_sum += weight * ext_ref[d, 1, g + tap + 1]
+            cos_phase, sin_phase = cos_ref[g], sin_ref[g]
+            compressed = jnp.concatenate(
+                [re_sum * cos_phase - im_sum * sin_phase, im_sum * cos_phase + re_sum * sin_phase],
+                axis=1,
+            ).astype(jnp.bfloat16)
+            first = dot(compressed, back_right_ref[...])
+            re, im = first[:, :LANES], first[:, LANES:]
+            tc, ts = tc_ref[...], ts_ref[...]
+            segment = jnp.concatenate([re * tc - im * ts, im * tc + re * ts], axis=0)
+            second = dot(back_left_ref[...], segment.astype(jnp.bfloat16)) * (1.0 / SPLIT)
+            second = second.astype(jnp.bfloat16)
+            if d == 0:
+                focused_ref[g] = second
+                return carry
+            leading, trailing = second.astype(jnp.float32), focused_ref[g].astype(jnp.float32)
+            lr, li = leading[:SPLIT], leading[SPLIT:]
+            tr, ti = trailing[:SPLIT], trailing[SPLIT:]
+            product = jnp.concatenate([lr * tr + li * ti, li * tr - lr * ti], axis=1)
+            high = product.astype(jnp.bfloat16)
+            high_ref[g] = high
+            low_ref[g] = (product - high.astype(jnp.float32)).astype(jnp.bfloat16)
+            return carry
+
+        lax.fori_loop(0, GROUPS, focus, 0, unroll=2)
 
     for d in range(dates):
 
@@ -329,64 +429,15 @@
 
         lax.fori_loop(0, GROUPS // 2, forward, 0, unroll=2)
         start_pair(edge_copies(d))
-
-    for d in range(dates):
-        wait_pair(edge_copies(d))
-
-        def fill(i, carry):
-            before = before_ref[d, i].astype(jnp.float32)
-            after = after_ref[d, i].astype(jnp.float32)
-            before_parts = (before, pltpu.roll(before, SPLIT, 1))
-            after_parts = (pltpu.roll(after, SPLIT, 1), after)
-            for c in range(2):
-                ext_ref[d, c, i] = jnp.where(low, before_parts[c], ext_ref[d, c, i])
-                last = i + 3 * SHIFT
-                ext_ref[d, c, last] = jnp.where(low, ext_ref[d, c, last], after_parts[c])
-            return carry
-
-        lax.fori_loop(0, SHIFT, fill, 0)
-
-    def focus(g, carry):
-        parts = []
-        for half in range(2):
-            rows = pl.ds(half * (SPLIT // 2), SPLIT // 2)
-            sums = [jnp.zeros((SPLIT // 2, LANES), jnp.float32) for _ in range(2 * dates)]
-            for tap in range(TAPS):
-                weight = weight_ref[g, tap, rows]
-                for d in range(dates):
-                    for c in range(2):
-                        sums[2 * d + c] += weight * ext_ref[d, c, g + tap + 1, rows]
-            cos_phase, sin_phase = cos_ref[g, rows], sin_ref[g, rows]
-            parts.append(
-                [
-                    jnp.concatenate(
-                        [
-                            sums[2 * d] * cos_phase - sums[2 * d + 1] * sin_phase,
-                            sums[2 * d + 1] * cos_phase + sums[2 * d] * sin_phase,
-                        ],
-                        axis=1,
-                    ).astype(jnp.bfloat16)
-                    for d in range(dates)
-                ]
-            )
-        focused = []
-        for d in range(dates):
-            compressed = jnp.concatenate([parts[0][d], parts[1][d]], axis=0)
-            first = dot(compressed, back_right_ref[...])
-            re, im = first[:, :LANES], first[:, LANES:]
-            tc, ts = tc_ref[...], ts_ref[...]
-            segment = jnp.concatenate([re * tc - im * ts, im * tc + re * ts], axis=0)
-            second = dot(back_left_ref[...], segment.astype(jnp.bfloat16)) * (1.0 / SPLIT)
-            second = second.astype(jnp.bfloat16).astype(jnp.float32)
-            focused.append((second[:SPLIT], second[SPLIT:]))
-        (tr, ti), (lr, li) = focused
-        product = jnp.concatenate([lr * tr + li * ti, li * tr - lr * ti], axis=1)
-        high = product.astype(jnp.bfloat16)
-        high_ref[g] = high
-        low_ref[g] = (product - high.astype(jnp.float32)).astype(jnp.bfloat16)
-        return carry
-
-    lax.fori_loop(0, GROUPS, focus, 0)
+        if d == 0:
+
+            def send_rest(o, carry):
+                strip_copy(1, o).start()
+                return carry
+
+            lax.fori_loop(held, scene, send_rest, 0)
+        focus_date(d)
+
     for big in range(GROUPS // 4):
         high = jnp.concatenate([high_ref[4 * big + j] for j in range(4)], axis=1)
         rest = jnp.concatenate([low_ref[4 * big + j] for j in range(4)], axis=1)
@@ -455,8 +506,7 @@
         stacked = jnp.concatenate([back[:, :LANES], back[:, LANES:]], axis=0)
         result = (dot(back_range_ref[...], stacked) * (1.0 / PATCH)).astype(jnp.bfloat16)
         start = pl.multiple_of(step * LANES, LANES)
-        for pair in range(out_ref.shape[0]):
-            out_ref[pair, :, pl.ds(start, LANES)] = result
+        out_ref[:, pl.ds(start, LANES)] = result
         return carry
 
     lax.fori_loop(0, patches // 4, filter_patches, 0)
@@ -470,9 +520,17 @@
         lax.fori_loop(1, scene, sent, 0)
 
 
-def run_scene(raw, band, phase, left, scene, pairs):
-    dates = raw.shape[1]
-    width = raw.shape[3]
+def loading_kernel(band_ref, *refs):
+    held, out_ref, kept, load_sem = refs[:TABLES], refs[TABLES], refs[TABLES + 1 : -1], refs[-1]
+    loads = [
+        pltpu.make_async_copy(source, target, load_sem.at[i])
+        for i, (source, target) in enumerate(zip(held, kept[:TABLES]))
+    ]
+    scene_kernel(band_ref, *kept[:TABLES], out_ref, *kept[TABLES:], loads)
+
+
+def run_scene(raw, band, phase, left, scene, shape):
+    dates, width = shape[1], shape[3]
     looks = SPLIT * SPLIT // LOOKS
     tc, ts = twiddle_tables()
     vmem = pl.BlockSpec(memory_space=pltpu.VMEM)
@@ -481,39 +539,46 @@
     looked_edge = pltpu.VMEM((HALO_CHUNKS, SPLIT, LANES), jnp.bfloat16)
     products = pltpu.VMEM((GROUPS, SPLIT, 2 * LANES), jnp.bfloat16)
     dma = pltpu.SemaphoreType.DMA
+    tables = (
+        raw, phase, bf16(left), bf16(spectrum_side(right_table(1.0), 1)),
+        bf16(spectrum_side(right_table(-1.0), 0)), bf16(left_table(-1.0)),
+        jnp.asarray(tc), jnp.asarray(ts), bf16(look_table()),
+        bf16(patch_azimuth_table()), bf16(patch_range_table()),
+        bf16(back_azimuth_table()), bf16(back_range_table()),
+    )
     return pl.pallas_call(
-        scene_kernel,
-        in_specs=[pl.BlockSpec(memory_space=pl.ANY), pl.BlockSpec(memory_space=pltpu.SMEM)]
-        + [vmem] * 12,
+        loading_kernel,
+        in_specs=[pl.BlockSpec(memory_space=pltpu.SMEM)]
+        + [pl.BlockSpec(memory_space=pl.ANY)] * TABLES,
         out_specs=vmem,
-        out_shape=jax.ShapeDtypeStruct((pairs, 2 * STRIP, looks), jnp.bfloat16),
-        scratch_shapes=[
+        out_shape=jax.ShapeDtypeStruct((2 * STRIP, looks), jnp.bfloat16),
+        scratch_shapes=[pltpu.VMEM(table.shape, table.dtype) for table in tables]
+        + [
+            pltpu.VMEM(shape, jnp.bfloat16),
+            pltpu.VMEM(raw.shape, jnp.float32),
             pltpu.VMEM((dates, scene, 2, STRIP, width), jnp.bfloat16),
+            pltpu.VMEM((STRIP * SPLIT // 2, LANES), jnp.float32),
             pltpu.VMEM((2, pl.cdiv(width, LANES), scene * STRIP, LANES), jnp.float32),
             pltpu.VMEM((GROUPS, TAPS, SPLIT, LANES), jnp.float32),
             pltpu.VMEM(plane, jnp.float32),
             pltpu.VMEM(plane, jnp.float32),
             pltpu.VMEM((dates, 2, GROUPS + 2 * SHIFT, SPLIT, LANES), jnp.float32),
-            edge, edge, edge, edge, products, products,
+            edge, edge, edge, edge,
+            pltpu.VMEM((GROUPS, 2 * SPLIT, LANES), jnp.bfloat16),
+            products, products,
             pltpu.VMEM((CHUNKS, SPLIT, LANES), jnp.bfloat16),
             looked_edge,
             looked_edge,
             pltpu.VMEM((2 * CHUNKS, SPLIT + 8, LANES), jnp.float32),
             pltpu.VMEM((PATCH * SPLIT // 2, LANES), jnp.float32),
             dma((dates, scene)), dma((dates, scene)), dma((dates,)),
-            dma((dates, 2)), dma((dates, 2)), dma((2,)), dma((2,)),
+            dma((dates, 2)), dma((dates, 2)), dma((2,)), dma((2,)), dma((TABLES,)),
         ],
         compiler_params=pltpu.CompilerParams(
             vmem_limit_bytes=VMEM_LIMIT, collective_id=0, has_side_effects=True
         ),
         name="scene",
-    )(
-        raw, band, phase, bf16(left), bf16(spectrum_side(right_table(1.0), 1)),
-        bf16(spectrum_side(right_table(-1.0), 0)), bf16(left_table(-1.0)),
-        jnp.asarray(tc), jnp.asarray(ts), bf16(look_table()),
-        bf16(patch_azimuth_table()), bf16(patch_range_table()),
-        bf16(back_azimuth_table()), bf16(back_range_table()),
-    )
+    )(band, *tables)
 
 
 def on_device(raw_echoes, azimuth_phase, band_offset, partners):
@@ -524,9 +589,14 @@
     assert dates == 2 and raw_echoes.shape[3] == scene * STRIP
     left = left_table(1.0).reshape(2 * SPLIT, 2, scene, local)
     left = left.transpose(0, 1, 3, 2).reshape(2 * SPLIT, 2 * SPLIT)
-    raw = raw_echoes.transpose(1, 2, 3, 0)
-    phase = azimuth_phase.T.reshape(STRIP, SPLIT // 2, LANES)
-    result = run_scene(raw, band_offset, phase, left, scene, pairs)
+    lines, bins = raw_echoes.shape[0], raw_echoes.shape[3]
+    raw = raw_echoes.reshape(lines, 2, dates, bins // LANES, LANES)
+    raw = raw.transpose(0, 1, 3, 2, 4).reshape(-1, LANES)
+    phase = azimuth_phase.T
+    result = run_scene(
+        raw, band_offset, phase, left, scene, (2, dates, bins, lines)
+    )
+    result = jnp.broadcast_to(result, (pairs,) + result.shape)
     return result.reshape(pairs, 2, STRIP, -1).transpose(0, 3, 1, 2)
 
 

time: 64.3 us -> 60.8 us (0.946)
  the two profiles are of different devices: /device:TPU:13 before, /device:TPU:18 now
where the time goes in v2:
time: 60.8 us; the launch traced here: 60 us
  Pallas kernels  58.4 us (96%)
  local copies, waits for them, and re-layouts  1.63 us (3%)
    pallas_call x1, Pallas kernels, run_scene(): pl.pallas_call(loading_kernel, in_specs=[pl.BlockSpec(memory_space=pltpu....  58.4 us
    transpose x1, local copies, waits for them, and re-layouts, on_device(): return result.reshape(pairs, 2, STRIP, -1).transpose(0, 3, 1, 2)  1.63 us

profile of v2, /device:TPU:18, one launch (start us, length us, event | category | flops | bytes accessed | tf_op | source)
XLA Modules:
  0.0 60.0 jit_solution(3839525912647035331)
XLA Ops:
  0.0 58.4 %scene.1 = bf16[64,1024]{1,0:T(8,128)(2,1)} custom-call(s32[32]{0:T(128)} %band_ref.1, bf16[4096,128]{1,0:T(8,128)(2,1)} %bitcast.9, f32[32,4096]{1,0:T(8,128)} %bitcast.11, bf16[128,128]{1,0:T(8,128)(2,1)} %constant.22.clone.refs_2_, bf16[256,256]{1,0:T(8,128)(2,1)} %constant.23.clone.refs_3_, bf16[256,256]{1,0:T(8,128)(2,1)} %constant.24.clone.refs_4_, ...), custom_call_target="tpu_custom_call" | custom-call | tf_op jit(solution)/shard_map/scene/pallas_call | solution.py:549
  58.4 1.6 %broadcast_bitcast_fusion = bf16[2,1024,2,32]{1,3,2,0:T(8,128)(2,1)} fusion(bf16[2,32,1024]{2,1,0:T(8,128)(2,1)} %bitcast.10), kind=kLoop, calls=%fused_computation | loop fusion | bytes 393216 | tf_op jit(solution)/shard_map/transpose | solution.py:600

commit v3 on v2

--- a/solution.py
+++ b/solution.py
@@ -382,7 +382,7 @@
             low_ref[g] = (product - high.astype(jnp.float32)).astype(jnp.bfloat16)
             return carry
 
-        lax.fori_loop(0, GROUPS, focus, 0, unroll=2)
+        lax.fori_loop(0, GROUPS, focus, 0, unroll=8)
 
     for d in range(dates):
 
@@ -427,7 +427,7 @@
                     up_ref[d, i] = jnp.where(low, re_turned, im).astype(jnp.bfloat16)
             return carry
 
-        lax.fori_loop(0, GROUPS // 2, forward, 0, unroll=2)
+        lax.fori_loop(0, GROUPS // 2, forward, 0, unroll=8)
         start_pair(edge_copies(d))
         if d == 0:
 
@@ -509,7 +509,7 @@
         out_ref[:, pl.ds(start, LANES)] = result
         return carry
 
-    lax.fori_loop(0, patches // 4, filter_patches, 0)
+    lax.fori_loop(0, patches // 4, filter_patches, 0, unroll=4)
 
     for d in range(dates):
 

time: 60.8 us -> 55.9 us (0.919); the launches traced: 60 us -> 55.8 us
  Pallas kernels: 58.4 us -> 54.1 us
    pallas_call x1, Pallas kernels: 58.4 us -> 54.1 us  [run_scene(): pl.pallas_call(loading_kernel, in_specs=[pl.BlockSpec(memory_space=pltpu....]
where the time goes in v3:
time: 55.9 us; the launch traced here: 55.8 us
  Pallas kernels  54.1 us (97%)
  local copies, waits for them, and re-layouts  1.63 us (3%)
    pallas_call x1, Pallas kernels, run_scene(): pl.pallas_call(loading_kernel, in_specs=[pl.BlockSpec(memory_space=pltpu....  54.1 us
    transpose x1, local copies, waits for them, and re-layouts, on_device(): return result.reshape(pairs, 2, STRIP, -1).transpose(0, 3, 1, 2)  1.63 us

profile of v3, /device:TPU:18, one launch (start us, length us, event | category | flops | bytes accessed | tf_op | source)
XLA Modules:
  0.0 55.8 jit_solution(16394388040174971952)
XLA Ops:
  0.0 54.1 %scene.1 = bf16[64,1024]{1,0:T(8,128)(2,1)} custom-call(s32[32]{0:T(128)} %band_ref.1, bf16[4096,128]{1,0:T(8,128)(2,1)} %bitcast.9, f32[32,4096]{1,0:T(8,128)} %bitcast.11, bf16[128,128]{1,0:T(8,128)(2,1)} %constant.22.clone.refs_2_, bf16[256,256]{1,0:T(8,128)(2,1)} %constant.23.clone.refs_3_, bf16[256,256]{1,0:T(8,128)(2,1)} %constant.24.clone.refs_4_, ...), custom_call_target="tpu_custom_call" | custom-call | tf_op jit(solution)/shard_map/scene/pallas_call | solution.py:549
  54.1 1.6 %broadcast_bitcast_fusion = bf16[2,1024,2,32]{1,3,2,0:T(8,128)(2,1)} fusion(bf16[2,32,1024]{2,1,0:T(8,128)(2,1)} %bitcast.10), kind=kLoop, calls=%fused_computation | loop fusion | bytes 393216 | tf_op jit(solution)/shard_map/transpose | solution.py:600
